TPU v7x, 32 devices: a whole 2x2x4 slice. The times are simulated.
32 devices in a mesh: groups: 2 (over x), pairs: 16 (over z, y, core).
Axes of the slice: x: 2, y: 2, z: 4, core: 2. Of those that a mesh axis runs over, the one named last changes fastest.
Arguments:
- traces: bfloat16 [128, 3, 4096], P(('groups', 'pairs')), parts along dimension 0, may hold values from -6 to 6
- gaps: int32 [128, 2], P(('groups', 'pairs')), parts along dimension 0, may hold values 0 or 1
- assign: int32 [128], P('groups'), parts along dimension 0, may hold values from 0 to 3, as said below
- target: int32 [32], P('groups'), parts along dimension 0, may hold values from 0 to 3, as said below
Outputs:
- correlations: bfloat16 [128, 16, 2, 9, 256], P(('groups', 'pairs')), parts along dimension 0
- energy: float32 [128, 9], P(('groups', 'pairs')), parts along dimension 0
There are 2 independent parts, one for each index of `groups`. A program takes and returns all parts, laid end to end along the dimension named above; each array names one. Nothing has to cross between parts.
Inputs may be any that keep to these rules, and one draw needn't show every extreme that they name: `assign`: the 4 stations of one owner name at most 2 stations of any block; in every draw one block takes exactly 2 stations of every owner. `target`: in every draw some owner names the block that takes 2 stations of every owner.
All inputs are finite; a program needn't handle non-finite values. No bound on the sum of `gaps` on one device may be relied on, other than what follows from the above.
Results may differ from a plain program's by a relative error of at most 0.0075.
Values may be sent and summed in bfloat16 or wider, within the bound.
No kernel may reach another device: no remote copies, remote signals or barrier semaphores. Data moves between devices by JAX's collectives and lax.ppermute only.
A program may use at most 128 MiB of HBM per device.

v0:
```python
import math
import jax
import jax.numpy as jnp
from jax import lax
from jax.sharding import PartitionSpec as P

SEG = 2048
FREQ = 512
FLO = 64
LAGS = 256
HALF = 21
CAP = 2


def dft_table():
    samples = jnp.arange(SEG, dtype=jnp.int32)[:, None]
    bins = FLO + jnp.arange(FREQ, dtype=jnp.int32)[None, :]
    phase = jnp.mod(samples * bins, SEG).astype(jnp.float32) * (2.0 * math.pi / SEG)
    return jnp.concatenate([jnp.cos(phase), -jnp.sin(phase)], axis=1).astype(jnp.bfloat16)


def lag_table():
    bins = FLO + jnp.arange(FREQ, dtype=jnp.int32)[:, None]
    shifts = jnp.arange(LAGS, dtype=jnp.int32)[None, :] - LAGS // 2
    phase = jnp.mod(bins * shifts, SEG).astype(jnp.float32) * (2.0 * math.pi / SEG)
    return jnp.concatenate([jnp.cos(phase), -jnp.sin(phase)], axis=0).astype(jnp.bfloat16)


def smooth_band():
    column = jnp.arange(FREQ, dtype=jnp.int32)
    band = (jnp.abs(column[:, None] - column[None, :]) <= HALF).astype(jnp.float32)
    return (band, jnp.sum(band, axis=0))


def whiten_all(traces, gaps):
    stations = traces.shape[0]
    windows = gaps.shape[1]
    segments = traces.reshape(stations * 3 * windows, SEG)
    spectra = jnp.dot(segments, dft_table(), preferred_element_type=jnp.float32)
    spectra = spectra.reshape(stations, 3, windows, 2, FREQ)
    power = jnp.sum(spectra * spectra, axis=(1, 3)) / 3.0
    band, bin_count = smooth_band()
    smooth = jnp.dot(power.reshape(-1, FREQ), band, precision=lax.Precision.HIGHEST)
    smooth = smooth.reshape(stations, windows, FREQ) / bin_count
    factor = gaps.astype(jnp.float32)[:, :, None] / jnp.sqrt(smooth + 1e-06)
    return (spectra * factor[:, None, :, None, :]).astype(jnp.bfloat16)


def station_ranks(owner_assign):
    own_count = owner_assign.shape[1]
    same = owner_assign[:, :, None] == owner_assign[:, None, :]
    order = jnp.arange(own_count, dtype=jnp.int32)
    before = order[:, None] < order[None, :]
    return jnp.sum((same & before[None, :, :]).astype(jnp.int32), axis=1)


def correlate_block(whitened, own_mask, partner, partner_mask, lag_tab):
    own_count = whitened.shape[0]
    slot_count = partner.shape[0]
    real_part = partner[:, :, :, 0]
    imag_part = partner[:, :, :, 1]
    quad = jnp.stack(
        [jnp.stack([real_part, imag_part], 3), jnp.stack([-imag_part, real_part], 3)], 4
    )
    cross = jnp.einsum("icwrf,jdwrof->ijcdof", whitened, quad, preferred_element_type=jnp.float32)
    cross = cross.astype(jnp.bfloat16)
    lagged = jnp.dot(cross.reshape(-1, 2 * FREQ), lag_tab, preferred_element_type=jnp.float32)
    lagged = lagged.reshape(own_count, slot_count, 9, LAGS)
    counts = jnp.dot(own_mask, partner_mask.T, precision=lax.Precision.HIGHEST)
    scale = 1.0 / (jnp.maximum(counts, 1.0) * math.sqrt(FREQ))
    return (lagged * scale[:, :, None, None]).astype(jnp.bfloat16)


def correlate_slots(whitened, own_mask, partner, partner_mask):
    own_count = whitened.shape[0]
    windows = whitened.shape[2]
    senders = partner.shape[0]
    width = partner.shape[1]
    stride = min(senders, 16)
    lag_tab = lag_table()
    initial = jnp.zeros((own_count, senders, width, 9, LAGS), jnp.bfloat16)

    def advance(position, filled):
        start = position * stride
        piece = lax.dynamic_slice_in_dim(partner, start, stride, 0)
        piece = piece.reshape(stride * width, 3, windows, 2, FREQ)
        mask_piece = lax.dynamic_slice_in_dim(partner_mask, start, stride, 0)
        mask_piece = mask_piece.reshape(stride * width, windows).astype(jnp.float32)
        result = correlate_block(whitened, own_mask, piece, mask_piece, lag_tab)
        result = result.reshape(own_count, stride, width, 9, LAGS)
        return lax.dynamic_update_slice_in_dim(filled, result, start, 1)

    return lax.fori_loop(0, senders // stride, advance, initial)


def on_device(traces, gaps, assign, target):
    whitened = whiten_all(traces, gaps)
    own_count = whitened.shape[0]
    owners = lax.axis_size("pairs")
    my_index = lax.axis_index("pairs")
    own_mask = gaps.astype(jnp.float32)
    station_rows = whitened.reshape(own_count, -1)
    mask_rows = gaps.astype(jnp.bfloat16)
    owner_assign = assign.reshape(owners, own_count)
    ranks = station_ranks(owner_assign)
    slot_ids = jnp.arange(CAP, dtype=jnp.int32)
    wanted = lax.dynamic_index_in_dim(target, my_index, 0, keepdims=False)
    select_in = (
        (owner_assign == wanted)[:, None, :] & (ranks[:, None, :] == slot_ids[None, :, None])
    ).astype(jnp.bfloat16)
    my_assign = lax.dynamic_index_in_dim(owner_assign, my_index, 0, keepdims=False)
    my_ranks = lax.dynamic_index_in_dim(ranks, my_index, 0, keepdims=False)
    select_out = (
        (my_assign[None, :] == target[:, None])[:, None, :]
        & (my_ranks[None, None, :] == slot_ids[None, :, None])
    ).astype(jnp.bfloat16)
    everyone, every_mask = (
        lax.all_gather(station_rows, "pairs", axis=0, tiled=True),
        lax.all_gather(mask_rows, "pairs", axis=0, tiled=True),
    )
    partner = jnp.einsum(
        "ecs,esr->ecr",
        select_in,
        everyone.reshape(owners, own_count, -1),
        preferred_element_type=jnp.float32,
    ).astype(jnp.bfloat16)
    partner_mask = jnp.einsum(
        "ecs,esw->ecw",
        select_in,
        every_mask.reshape(owners, own_count, -1),
        preferred_element_type=jnp.float32,
    ).astype(jnp.bfloat16)
    correlations = correlate_slots(whitened, own_mask, partner, partner_mask)
    slot_energy = jnp.sum(jnp.square(correlations.astype(jnp.float32)), axis=(0, 4))
    returned = lax.all_to_all(slot_energy, "pairs", split_axis=0, concat_axis=0, tiled=True)
    energy = jnp.einsum(
        "pcs,pcq->sq", select_out.astype(jnp.float32), returned, precision=lax.Precision.HIGHEST
    )
    energy = energy / float(owners * LAGS)
    return (correlations, energy)


def solution(mesh):
    in_specs = (
        P(("groups", "pairs"), None, None),
        P(("groups", "pairs"), None),
        P("groups"),
        P("groups"),
    )
    out_specs = (P(("groups", "pairs"), None, None, None, None), P(("groups", "pairs"), None))
    return jax.shard_map(
        on_device, mesh=mesh, in_specs=in_specs, out_specs=out_specs, check_vma=False
    )
```

profile of v0, /device:TPU:0, one launch (start us, length us, event | category | flops | bytes accessed | tf_op | source)
XLA Modules:
  0.0 122.6 jit_solution(12688342774132318976)
XLA Ops:
  0.7 0.1 convert_reduce_fusion
  0.8 1.0 copy.74
  1.7 0.1 reshape.137
  1.8 17.0 %cosine_convert_fusion = (bf16[2048,512]{1,0:T(8,128)(2,1)S(1)}, bf16[2048,512]{1,0:T(8,128)(2,1)S(1)}) fusion(s32[512]{0:T(512)S(1)} %iota_add_fusion), kind=kLoop, calls=%fused_computation.14 | loop fusion | flops 17825792 | bytes 4196352 | tf_op jit(solution)/shard_map/convert.2
  18.8 0.0 copy-start.1
  18.8 0.0 copy-start.2
  18.9 0.0 copy-start.3
  18.9 0.6 fusion.14
  19.5 0.1 reshape.139
  19.6 0.1 reshape.138
  19.7 0.1 reshape.136
  19.8 0.1 copy.71
  19.9 0.6 dynamic_slice.17
  20.5 0.6 broadcast_compare_fusion
  21.1 0.1 convert_reduce_fusion.1
  21.2 0.1 copy.73
  21.3 0.1 multiply_reduce_fusion.1
  21.4 0.3 fusion.19
  21.8 0.1 mul.96
  22.0 25.5 %all-gather = bf16[16,4,6144]{2,1,0:T(4,128)(2,1)S(1)} all-gather(bf16[1,4,6144]{2,1,0:T(4,128)(2,1)S(1)} %fusion.31), channel_id=1, replica_groups=mesh['groups'=2,'pairs'=16] {'pairs'}, dimensions={0}, use_global_device_ids=true | all-gather | bytes 835584 | tf_op jit(solution)/shard_map/all_gather | solution.py:118
  47.5 0.6 convolution_convert_fusion
  48.0 0.2 reshape.141
  48.3 0.2 stack.20
  48.5 0.5 iota_add_fusion.1
  49.1 17.4 %all-gather.1 = bf16[16,4,2]{1,2,0:T(2,128)(2,1)S(1)} all-gather(bf16[1,4,2]{1,2,0:T(2,128)(2,1)S(1)} %get-tuple-element.44), channel_id=1, replica_groups=mesh['groups'=2,'pairs'=16] {'pairs'}, dimensions={0}, use_global_device_ids=true | all-gather | bytes 272 | tf_op jit(solution)/shard_map/all_gather | solution.py:119
  66.5 0.1 convolution_convert_fusion.1
  66.7 0.8 fusion.22
  67.4 1.7 %copy.88 = bf16[4,3,2,2,512,1,1]{0,2,3,1,6,5,4:T(2,128)(2,1)S(1)} copy(bf16[4,3,2,2,512,1,1]{4,3,2,1,0,6,5:T(2,128)(2,1)S(1)} %fusion.32) | data formatting | bytes 98304 | tf_op jit(solution)/shard_map/convert_element_type | solution.py:46
  69.2 0.5 fusion.48
  69.7 0.1 copy.95
  69.8 0.1 copy_negate_fusion
  69.9 0.8 pad_maximum_fusion
  70.7 3.5 %copy.79 = bf16[32,3,2,2,512]{0,2,3,1,4:T(2,128)(2,1)S(1)} copy(bf16[32,3,2,2,512]{4,0,3,2,1:T(8,128)(2,1)} %pad_maximum_fusion) | data formatting | bytes 786432 | tf_op jit(solution)/shard_map/while/body/eval_jaxpr/stack | solution.py:63
  74.2 3.1 %copy.80 = bf16[32,3,2,2,1,512]{0,2,3,4,1,5:T(2,128)(2,1)} copy(bf16[32,3,2,2,1,512]{5,3,2,1,0,4:T(2,128)(2,1)S(1)} %stack.20) | data formatting | bytes 786432 | tf_op jit(solution)/shard_map/while/body/eval_jaxpr/stack | solution.py:62
  77.3 11.5 %fusion = bf16[4,32,3,3,2,512]{1,0,2,4,3,5:T(4,128)(2,1)} fusion(bf16[4,3,2,2,512,1,1]{0,2,3,1,6,5,4:T(2,128)(2,1)S(1)} %copy.88, bf16[32,3,2,2,1,512]{0,2,3,4,1,5:T(2,128)(2,1)S(1)} %bitcast.54, bf16[32,3,2,2,1,512]{0,2,3,4,1,5:T(2,128)(2,1)} %copy.80), kind=kOutput, calls=%fused_computation.1 | convolution fusion | flops 12189696 | bytes 3194880 | tf_op jit(solution)/shard_map/while/body/eval_jaxpr/icwrf,jdwrof->ijcdof/dot_general | solution.py:65
  88.8 14.3 %copy.82 = bf16[4,32,3,3,2,512]{5,4,1,3,2,0:T(2,128)(2,1)S(1)} copy(bf16[4,32,3,3,2,512]{1,0,2,4,3,5:T(4,128)(2,1)} %fusion) | data formatting | bytes 4718592 | tf_op jit(solution)/shard_map/while/body/eval_jaxpr/convert_element_type | solution.py:66
  103.1 0.0 copy-start.5
  103.1 2.9 %dot_general.36 = bf16[4,32,9,1024]{3,1,2,0:T(8,128)(2,1)} reshape(bf16[4,32,3,3,2,512]{5,4,1,3,2,0:T(2,128)(2,1)S(1)} %copy.82) | data formatting | bytes 4718592 | tf_op jit(solution)/shard_map/while/body/eval_jaxpr/dot_general | solution.py:67
  106.1 2.5 %cosine_convert_fusion.1 = (bf16[512,256]{1,0:T(8,128)(2,1)S(1)}, bf16[512,256]{1,0:T(8,128)(2,1)S(1)}) fusion(s32[256]{0:T(256)S(1)} %copy-done, s32[512]{0:T(512)S(1)} %iota_add_fusion), kind=kLoop, calls=%fused_computation.51 | loop fusion | flops 2228224 | bytes 527360 | tf_op jit(solution)/shard_map/convert
  108.6 2.5 %multiply_reduce_fusion = (f32[32,9]{0,1:T(8,128)S(1)}, bf16[4,32,9,256]{3,1,2,0:T(8,128)(2,1)S(1)}) fusion(f32[4,32]{1,0:T(4,128)S(1)} %copy-done.5, bf16[4,32,9,1024]{3,1,2,0:T(8,128)(2,1)} %dot_general.36, bf16[512,256]{1,0:T(8,128)(2,1)S(1)} %get-tuple-element.41, bf16[512,256]{1,0:T(8,128)(2,1)S(1)} %get-tuple-element.40), kind=kOutput, calls=%fused_computation.23 | convolution fusion | flops 606502656 | bytes 3475072 | tf_op jit(solution)/shard_map/while/body/eval_jaxpr/dot_general | solution.py:67
  111.1 0.7 copy.84
  111.8 3.5 %all-to-all-start = ((f32[16,2,9]{2,1,0:T(2,128)}), f32[16,2,9]{2,1,0:T(2,128)S(1)}, u32[]{:S(2)}, u32[]{:S(2)}) async-start(f32[16,2,9]{2,1,0:T(2,128)} %bitcast.17), calls=%async_computation | async-start | bytes 32768 | tf_op jit(solution)/shard_map/all_to_all | solution.py:135
  115.3 0.2 dynamic-slice_reduce_fusion
  115.5 0.1 broadcast_compare_fusion.1
  115.6 0.2 reshape.144
  115.8 1.2 copy.86
  117.0 4.7 %all-to-all-done = f32[16,2,9]{2,1,0:T(2,128)S(1)} async-done(((f32[16,2,9]{2,1,0:T(2,128)}), f32[16,2,9]{2,1,0:T(2,128)S(1)}, u32[]{:S(2)}, u32[]{:S(2)}) %all-to-all-start) | async-done | bytes 1184 | tf_op jit(solution)/shard_map/all_to_all | solution.py:135
  121.7 0.8 fusion.23
  (17 shorter events, 0.2 us)
Async XLA Ops:
  18.8 0.9 copy-start.1
  18.8 0.9 copy-start.2
  18.9 1.0 copy-start.3
  103.1 2.9 %copy-start = (s32[256]{0:T(256)S(1)}, s32[256]{0:T(256)}, u32[]{:S(2)}) copy-start(s32[256]{0:T(256)} %iota_add_fusion.1) | copy-start | bytes 3076
  103.1 5.4 %copy-start.5 = (f32[4,32]{1,0:T(4,128)S(1)}, f32[4,32]{1,0:T(4,128)}, u32[]{:S(2)}) copy-start(f32[4,32]{1,0:T(4,128)} %fusion.22) | copy-start | bytes 1540
  106.0 9.4 %copy-start.4 = (s32[16]{0:T(128)S(1)}, s32[16]{0:T(128)}, u32[]{:S(2)}) copy-start(s32[16]{0:T(128)} %param.7) | copy-start | bytes 196
  111.8 10.0 %all-to-all-start = ((f32[16,2,9]{2,1,0:T(2,128)}), f32[16,2,9]{2,1,0:T(2,128)S(1)}, u32[]{:S(2)}, u32[]{:S(2)}) async-start(f32[16,2,9]{2,1,0:T(2,128)} %bitcast.17), calls=%async_computation | async-start | bytes 32768 | tf_op jit(solution)/shard_map/all_to_all | solution.py:135
where the time goes:
time: 123 us
  blocking collectives  42.9 us (35%)
  local copies, waits for them, and re-layouts  31.3 us (25%)
  other arithmetic  21.9 us (18%)
  matrix products  17.3 us (14%)
  waiting for transfers between devices  4.73 us (4%)
  starting transfers between devices  3.49 us (3%)
    all_gather x1, blocking collectives, on_device(): lax.all_gather(station_rows, 'pairs', axis=0, tiled=True)  25.5 us
    another operation x2, other arithmetic  19.5 us
    all_gather x1, blocking collectives, on_device(): lax.all_gather(mask_rows, 'pairs', axis=0, tiled=True)  17.4 us
    convert_element_type x1, local copies, waits for them, and re-layouts, correlate_block(): cross = cross.astype(jnp.bfloat16)  14.3 us
    dot_general x1, matrix products, correlate_block(): jnp.einsum('icwrf,jdwrof->ijcdof', whitened, quad, preferred_element_type...  11.5 us
    all_to_all x1, waiting for transfers between devices, on_device(): lax.all_to_all(slot_energy, 'pairs', split_axis=0, concat_axis=0, tiled=T...  4.73 us
    another operation x1, local copies, waits for them, and re-layouts, correlate_block(): jnp.stack([-imag_part, real_part], 3)  3.52 us
    all_to_all x1, starting transfers between devices, on_device(): lax.all_to_all(slot_energy, 'pairs', split_axis=0, concat_axis=0, tiled=T...  3.49 us
  transfers between devices with their start and end apart: 1, of which 1 were waited for; matrix products, arithmetic and copies ran while one was open for 1% of the time, Pallas kernels for 0%

commit v1 on v0

--- a/solution.py
+++ b/solution.py
@@ -10,6 +10,19 @@
 LAGS = 256
 HALF = 21
 CAP = 2
+
+
+def gather_around(value, axis, dim):
+    size, mine, width = (lax.axis_size(axis), lax.axis_index(axis), value.shape[dim])
+    right = [(i, (i + 1) % size) for i in range(size)]
+    result = jnp.zeros((*value.shape[:dim], size * width, *value.shape[dim + 1 :]), value.dtype)
+    block = value
+    for turn in range(size):
+        source = (mine - turn) % size
+        result = lax.dynamic_update_slice_in_dim(result, block, source * width, axis=dim)
+        if turn < size - 1:
+            block = lax.ppermute(block, axis, right)
+    return result
 
 
 def dft_table():
@@ -116,7 +129,7 @@
     ).astype(jnp.bfloat16)
     everyone, every_mask = (
         lax.all_gather(station_rows, "pairs", axis=0, tiled=True),
-        lax.all_gather(mask_rows, "pairs", axis=0, tiled=True),
+        gather_around(mask_rows, "pairs", 0),
     )
     partner = jnp.einsum(
         "ecs,esr->ecr",

time: 123 us -> 185 us (1.50)
  waiting for transfers between devices: 4.73 us -> 81.5 us
  blocking collectives: 42.9 us -> 24.8 us
    ppermute x0 -> x15, waiting for transfers between devices: none -> 76.5 us  [gather_around(): block = lax.ppermute(block, axis, right)]
    all_gather x1 -> x0, blocking collectives: 17.4 us -> none  [on_device(): lax.all_gather(mask_rows, 'pairs', axis=0, tiled=True)]
    dynamic_update_slice x0 -> x16, local copies, waits for them, and re-layouts: none -> 3.01 us  [gather_around(): lax.dynamic_update_slice_in_dim(result, block, source * width, axis=dim)]
    another operation x1, local copies, waits for them, and re-layouts: 3.52 us -> 1.54 us  [correlate_block(): jnp.stack([-imag_part, real_part], 3)]
  transfers between devices with their start and end apart: 1 -> 16, of which waited for: 1 -> 15; matrix products, arithmetic and copies ran while one was open for 1% -> 36% of each run, Pallas kernels for 0% -> 0%
where the time goes in v1:
time: 185 us; the launch traced here: 184 us
  waiting for transfers between devices  81.5 us (44%)
  local copies, waits for them, and re-layouts  31.4 us (17%)
  blocking collectives  24.8 us (13%)
  other arithmetic  22.6 us (12%)
  matrix products  18.4 us (10%)
  starting transfers between devices  4.49 us (2%)
    ppermute x15, waiting for transfers between devices, gather_around(): block = lax.ppermute(block, axis, right)  76.5 us
    all_gather x1, blocking collectives, on_device(): lax.all_gather(station_rows, 'pairs', axis=0, tiled=True)  24.8 us
    another operation x2, other arithmetic  20.6 us
    convert_element_type x1, local copies, waits for them, and re-layouts, correlate_block(): cross = cross.astype(jnp.bfloat16)  14.3 us
    dot_general x1, matrix products, correlate_block(): jnp.einsum('icwrf,jdwrof->ijcdof', whitened, quad, preferred_element_type...  11.5 us
    all_to_all x1, waiting for transfers between devices, on_device(): lax.all_to_all(slot_energy, 'pairs', split_axis=0, concat_axis=0, tiled=T...  5 us
  transfers between devices with their start and end apart: 16, of which 15 were waited for; matrix products, arithmetic and copies ran while one was open for 36% of the time, Pallas kernels for 0%

profile of v1, /device:TPU:0, one launch (start us, length us, event | category | flops | bytes accessed | tf_op | source)
XLA Modules:
  0.0 184.2 jit_solution(6626903638414857391)
XLA Ops:
  0.6 0.8 fusion.50
  1.4 0.5 collective-permute-start
  2.0 18.2 %cosine_convert_fusion = (bf16[2048,512]{1,0:T(8,128)(2,1)S(1)}, bf16[2048,512]{1,0:T(8,128)(2,1)}) fusion(s32[512]{0:T(512)S(1)} %iota_add_fusion), kind=kLoop, calls=%fused_computation.14 | loop fusion | flops 17825792 | bytes 4196352 | tf_op jit(solution)/shard_map/convert.2
  20.4 2.2 %fusion.14 = f32[24,1024]{1,0:T(8,128)S(1)} fusion(bf16[24,2048]{1,0:T(8,128)(2,1)S(1)} %reshape.137, bf16[2048,512]{1,0:T(8,128)(2,1)} %get-tuple-element.43, bf16[2048,512]{1,0:T(8,128)(2,1)S(1)} %get-tuple-element.42), kind=kOutput, calls=%fused_computation.24 | convolution fusion | flops 109051904 | bytes 4390912 | tf_op jit(solution)/shard_map/dot_general | solution.py:52
  23.0 0.6 dynamic_slice.17
  23.6 0.6 broadcast_compare_fusion
  24.5 0.3 fusion.19
  25.0 24.8 %all-gather = bf16[16,4,6144]{2,1,0:T(4,128)(2,1)S(1)} all-gather(bf16[1,4,6144]{2,1,0:T(4,128)(2,1)S(1)} %fusion.31), channel_id=1, replica_groups=mesh['groups'=2,'pairs'=16] {'pairs'}, dimensions={0}, use_global_device_ids=true | all-gather | bytes 835584 | tf_op jit(solution)/shard_map/all_gather | solution.py:131
  49.8 0.6 convolution_convert_fusion
  50.4 0.2 reshape.141
  50.7 0.2 stack.20
  51.2 0.5 fusion.49
  51.9 1.5 copy.84
  53.5 3.1 %copy.85 = bf16[32,3,2,2,1,512]{0,2,3,4,1,5:T(2,128)(2,1)} copy(bf16[32,3,2,2,1,512]{5,3,2,1,0,4:T(2,128)(2,1)S(1)} %stack.20) | data formatting | bytes 786432 | tf_op jit(solution)/shard_map/while/body/eval_jaxpr/stack | solution.py:75
  56.5 1.7 copy.94
  58.3 11.5 %fusion = bf16[4,32,3,3,2,512]{1,0,2,4,3,5:T(4,128)(2,1)} fusion(bf16[4,3,2,2,512,1,1]{0,2,3,1,6,5,4:T(2,128)(2,1)S(1)} %copy.94, bf16[32,3,2,2,1,512]{0,2,3,4,1,5:T(2,128)(2,1)S(1)} %bitcast.53, bf16[32,3,2,2,1,512]{0,2,3,4,1,5:T(2,128)(2,1)} %copy.85), kind=kOutput, calls=%fused_computation.1 | convolution fusion | flops 12189696 | bytes 3194880 | tf_op jit(solution)/shard_map/while/body/eval_jaxpr/icwrf,jdwrof->ijcdof/dot_general | solution.py:78
  69.8 14.3 %copy.87 = bf16[4,32,3,3,2,512]{5,4,1,3,2,0:T(2,128)(2,1)S(1)} copy(bf16[4,32,3,3,2,512]{1,0,2,4,3,5:T(4,128)(2,1)} %fusion) | data formatting | bytes 4718592 | tf_op jit(solution)/shard_map/while/body/eval_jaxpr/convert_element_type | solution.py:79
  84.2 2.9 %dot_general.36 = bf16[4,32,9,1024]{3,1,2,0:T(8,128)(2,1)} reshape(bf16[4,32,3,3,2,512]{5,4,1,3,2,0:T(2,128)(2,1)S(1)} %copy.87) | data formatting | bytes 4718592 | tf_op jit(solution)/shard_map/while/body/eval_jaxpr/dot_general | solution.py:80
  87.0 2.5 %cosine_convert_fusion.1 = (bf16[512,256]{1,0:T(8,128)(2,1)S(1)}, bf16[512,256]{1,0:T(8,128)(2,1)S(1)}) fusion(s32[256]{0:T(256)S(1)} %iota_add_fusion.1, s32[512]{0:T(512)S(1)} %iota_add_fusion), kind=kLoop, calls=%fused_computation.51 | loop fusion | flops 2228224 | bytes 527360 | tf_op jit(solution)/shard_map/convert
  89.8 0.5 collective-permute-start.1
  90.3 0.2 dynamic_update_slice.51
  90.5 5.1 %collective-permute-done.1 = bf16[4,2]{0,1:T(2,128)(2,1)S(1)} collective-permute-done((bf16[4,2]{0,1:T(2,128)(2,1)S(1)}, bf16[4,2]{0,1:T(2,128)(2,1)S(1)}, u32[]{:S(2)}, u32[]{:S(2)}) %collective-permute-start.1) | collective-permute-done | bytes 48 | tf_op jit(solution)/shard_map/ppermute | solution.py:24
  95.6 0.2 dynamic_update_slice.52
  95.8 5.5 %collective-permute-done.2 = bf16[4,2]{0,1:T(2,128)(2,1)S(1)} collective-permute-done((bf16[4,2]{0,1:T(2,128)(2,1)S(1)}, bf16[4,2]{0,1:T(2,128)(2,1)S(1)}, u32[]{:S(2)}, u32[]{:S(2)}) %collective-permute-start.2) | collective-permute-done | bytes 48 | tf_op jit(solution)/shard_map/ppermute | solution.py:24
  101.3 0.2 dynamic_update_slice.53
  101.5 5.5 %collective-permute-done.3 = bf16[4,2]{0,1:T(2,128)(2,1)S(1)} collective-permute-done((bf16[4,2]{0,1:T(2,128)(2,1)S(1)}, bf16[4,2]{0,1:T(2,128)(2,1)S(1)}, u32[]{:S(2)}, u32[]{:S(2)}) %collective-permute-start.3) | collective-permute-done | bytes 48 | tf_op jit(solution)/shard_map/ppermute | solution.py:24
  107.0 0.2 dynamic_update_slice.54
  107.1 5.5 %collective-permute-done.4 = bf16[4,2]{0,1:T(2,128)(2,1)S(1)} collective-permute-done((bf16[4,2]{0,1:T(2,128)(2,1)S(1)}, bf16[4,2]{0,1:T(2,128)(2,1)S(1)}, u32[]{:S(2)}, u32[]{:S(2)}) %collective-permute-start.4) | collective-permute-done | bytes 48 | tf_op jit(solution)/shard_map/ppermute | solution.py:24
  112.6 0.2 dynamic_update_slice.55
  112.8 5.5 %collective-permute-done.5 = bf16[4,2]{0,1:T(2,128)(2,1)S(1)} collective-permute-done((bf16[4,2]{0,1:T(2,128)(2,1)S(1)}, bf16[4,2]{0,1:T(2,128)(2,1)S(1)}, u32[]{:S(2)}, u32[]{:S(2)}) %collective-permute-start.5) | collective-permute-done | bytes 48 | tf_op jit(solution)/shard_map/ppermute | solution.py:24
  118.3 0.2 dynamic_update_slice.56
  118.5 5.5 %collective-permute-done.6 = bf16[4,2]{0,1:T(2,128)(2,1)S(1)} collective-permute-done((bf16[4,2]{0,1:T(2,128)(2,1)S(1)}, bf16[4,2]{0,1:T(2,128)(2,1)S(1)}, u32[]{:S(2)}, u32[]{:S(2)}) %collective-permute-start.6) | collective-permute-done | bytes 48 | tf_op jit(solution)/shard_map/ppermute | solution.py:24
  124.0 0.2 dynamic_update_slice.57
  124.2 5.5 %collective-permute-done.7 = bf16[4,2]{0,1:T(2,128)(2,1)S(1)} collective-permute-done((bf16[4,2]{0,1:T(2,128)(2,1)S(1)}, bf16[4,2]{0,1:T(2,128)(2,1)S(1)}, u32[]{:S(2)}, u32[]{:S(2)}) %collective-permute-start.7) | collective-permute-done | bytes 48 | tf_op jit(solution)/shard_map/ppermute | solution.py:24
  129.9 5.5 %collective-permute-done.8 = bf16[4,2]{0,1:T(2,128)(2,1)S(1)} collective-permute-done((bf16[4,2]{0,1:T(2,128)(2,1)S(1)}, bf16[4,2]{0,1:T(2,128)(2,1)S(1)}, u32[]{:S(2)}, u32[]{:S(2)}) %collective-permute-start.8) | collective-permute-done | bytes 48 | tf_op jit(solution)/shard_map/ppermute | solution.py:24
  135.6 5.5 %collective-permute-done.9 = bf16[4,2]{0,1:T(2,128)(2,1)S(1)} collective-permute-done((bf16[4,2]{0,1:T(2,128)(2,1)S(1)}, bf16[4,2]{0,1:T(2,128)(2,1)S(1)}, u32[]{:S(2)}, u32[]{:S(2)}) %collective-permute-start.9) | collective-permute-done | bytes 48 | tf_op jit(solution)/shard_map/ppermute | solution.py:24
  141.3 5.5 %collective-permute-done.10 = bf16[4,2]{0,1:T(2,128)(2,1)S(1)} collective-permute-done((bf16[4,2]{0,1:T(2,128)(2,1)S(1)}, bf16[4,2]{0,1:T(2,128)(2,1)S(1)}, u32[]{:S(2)}, u32[]{:S(2)}) %collective-permute-start.10) | collective-permute-done | bytes 48 | tf_op jit(solution)/shard_map/ppermute | solution.py:24
  147.0 5.5 %collective-permute-done.11 = bf16[4,2]{0,1:T(2,128)(2,1)S(1)} collective-permute-done((bf16[4,2]{0,1:T(2,128)(2,1)S(1)}, bf16[4,2]{0,1:T(2,128)(2,1)S(1)}, u32[]{:S(2)}, u32[]{:S(2)}) %collective-permute-start.11) | collective-permute-done | bytes 48 | tf_op jit(solution)/shard_map/ppermute | solution.py:24
  152.7 5.5 %collective-permute-done.12 = bf16[4,2]{0,1:T(2,128)(2,1)S(1)} collective-permute-done((bf16[4,2]{0,1:T(2,128)(2,1)S(1)}, bf16[4,2]{0,1:T(2,128)(2,1)S(1)}, u32[]{:S(2)}, u32[]{:S(2)}) %collective-permute-start.12) | collective-permute-done | bytes 48 | tf_op jit(solution)/shard_map/ppermute | solution.py:24
  158.4 5.5 %collective-permute-done.13 = bf16[4,2]{0,1:T(2,128)(2,1)S(1)} collective-permute-done((bf16[4,2]{0,1:T(2,128)(2,1)S(1)}, bf16[4,2]{0,1:T(2,128)(2,1)S(1)}, u32[]{:S(2)}, u32[]{:S(2)}) %collective-permute-start.13) | collective-permute-done | bytes 48 | tf_op jit(solution)/shard_map/ppermute | solution.py:24
  164.1 5.5 %collective-permute-done.14 = bf16[4,2]{0,1:T(2,128)(2,1)S(1)} collective-permute-done((bf16[4,2]{0,1:T(2,128)(2,1)S(1)}, bf16[4,2]{0,1:T(2,128)(2,1)S(1)}, u32[]{:S(2)}, u32[]{:S(2)}) %collective-permute-start.14) | collective-permute-done | bytes 48 | tf_op jit(solution)/shard_map/ppermute | solution.py:24
  170.2 2.6 %multiply_reduce_fusion = (f32[32,9]{0,1:T(8,128)S(1)}, bf16[4,32,9,256]{3,1,2,0:T(8,128)(2,1)S(1)}) fusion(f32[4,32]{1,0:T(4,128)S(1)} %fusion.22, bf16[4,32,9,1024]{3,1,2,0:T(8,128)(2,1)} %dot_general.36, bf16[512,256]{1,0:T(8,128)(2,1)S(1)} %get-tuple-element.41, bf16[512,256]{1,0:T(8,128)(2,1)S(1)} %get-tuple-element.40), kind=kOutput, calls=%fused_computation.23 | convolution fusion | flops 606502656 | bytes 3475072 | tf_op jit(solution)/shard_map/while/body/eval_jaxpr/dot_general | solution.py:80
  172.7 0.7 copy.90
  173.4 3.5 %all-to-all-start = ((f32[16,2,9]{2,1,0:T(2,128)}), f32[16,2,9]{2,1,0:T(2,128)S(1)}, u32[]{:S(2)}, u32[]{:S(2)}) async-start(f32[16,2,9]{2,1,0:T(2,128)} %bitcast.16), calls=%async_computation | async-start | bytes 32768 | tf_op jit(solution)/shard_map/all_to_all | solution.py:148
  176.9 0.2 reshape.144
  177.2 1.2 copy.92
  178.4 5.0 %all-to-all-done = f32[16,2,9]{2,1,0:T(2,128)S(1)} async-done(((f32[16,2,9]{2,1,0:T(2,128)}), f32[16,2,9]{2,1,0:T(2,128)S(1)}, u32[]{:S(2)}, u32[]{:S(2)}) %all-to-all-start) | async-done | bytes 1184 | tf_op jit(solution)/shard_map/all_to_all | solution.py:148
  183.4 0.8 fusion.23
  (60 shorter events, 3.7 us)
Async XLA Ops:
  0.6 19.5 %copy-start = (bf16[4,3,4096]{2,0,1:T(4,128)(2,1)S(1)}, bf16[4,3,4096]{2,0,1:T(4,128)(2,1)}, u32[]{:S(2)}) copy-start(bf16[4,3,4096]{2,0,1:T(4,128)(2,1)} %param.4) | copy-start | bytes 294916
  1.4 88.4 %collective-permute-start = (bf16[4,2]{0,1:T(2,128)(2,1)S(1)}, bf16[4,2]{0,1:T(2,128)(2,1)S(1)}, u32[]{:S(2)}, u32[]{:S(2)}) collective-permute-start(bf16[4,2]{0,1:T(2,128)(2,1)S(1)} %get-tuple-element.44), channel_id=1, source_target_pairs={{0,1},{1,2},{2,3},{3,4},{4,5},{5,6},{6,7},{7,8},{8,9},{9,10},{10,1... | collective-permute-start | bytes 56 | tf_op jit(solution)/shard_map/ppermute | solution.py:24
  20.4 2.4 %copy-start.2 = (s32[64]{0:T(128)S(1)}, s32[64]{0:T(128)}, u32[]{:S(2)}) copy-start(s32[64]{0:T(128)} %param.6) | copy-start | bytes 772
  20.4 2.6 %copy-start.3 = (s32[16]{0:T(128)S(1)}, s32[16]{0:T(128)}, u32[]{:S(2)}) copy-start(s32[16]{0:T(128)} %param.7) | copy-start | bytes 196
  84.1 85.9 %copy-start.1 = (s32[4,2]{0,1:T(2,128)S(1)}, s32[4,2]{0,1:T(2,128)}, u32[]{:S(2)}) copy-start(s32[4,2]{0,1:T(2,128)} %param.5) | copy-start | bytes 100
  89.8 5.7 %collective-permute-start.1 = (bf16[4,2]{0,1:T(2,128)(2,1)S(1)}, bf16[4,2]{0,1:T(2,128)(2,1)S(1)}, u32[]{:S(2)}, u32[]{:S(2)}) collective-permute-start(bf16[4,2]{0,1:T(2,128)(2,1)S(1)} %collective-permute-done), channel_id=1, source_target_pairs={{0,1},{1,2},{2,3},{3,4},{4,5},{5,6},{6,7},{7,8},{8,9},{9,10},{10,1... | collective-permute-start | bytes 56 | tf_op jit(solution)/shard_map/ppermute | solution.py:24
  95.6 5.7 %collective-permute-start.2 = (bf16[4,2]{0,1:T(2,128)(2,1)S(1)}, bf16[4,2]{0,1:T(2,128)(2,1)S(1)}, u32[]{:S(2)}, u32[]{:S(2)}) collective-permute-start(bf16[4,2]{0,1:T(2,128)(2,1)S(1)} %collective-permute-done.1), channel_id=1, source_target_pairs={{0,1},{1,2},{2,3},{3,4},{4,5},{5,6},{6,7},{7,8},{8,9},{9,10},{10,1... | collective-permute-start | bytes 56 | tf_op jit(solution)/shard_map/ppermute | solution.py:24
  101.3 5.7 %collective-permute-start.3 = (bf16[4,2]{0,1:T(2,128)(2,1)S(1)}, bf16[4,2]{0,1:T(2,128)(2,1)S(1)}, u32[]{:S(2)}, u32[]{:S(2)}) collective-permute-start(bf16[4,2]{0,1:T(2,128)(2,1)S(1)} %collective-permute-done.2), channel_id=1, source_target_pairs={{0,1},{1,2},{2,3},{3,4},{4,5},{5,6},{6,7},{7,8},{8,9},{9,10},{10,1... | collective-permute-start | bytes 56 | tf_op jit(solution)/shard_map/ppermute | solution.py:24
  107.0 5.7 %collective-permute-start.4 = (bf16[4,2]{0,1:T(2,128)(2,1)S(1)}, bf16[4,2]{0,1:T(2,128)(2,1)S(1)}, u32[]{:S(2)}, u32[]{:S(2)}) collective-permute-start(bf16[4,2]{0,1:T(2,128)(2,1)S(1)} %collective-permute-done.3), channel_id=1, source_target_pairs={{0,1},{1,2},{2,3},{3,4},{4,5},{5,6},{6,7},{7,8},{8,9},{9,10},{10,1... | collective-permute-start | bytes 56 | tf_op jit(solution)/shard_map/ppermute | solution.py:24
  112.6 5.7 %collective-permute-start.5 = (bf16[4,2]{0,1:T(2,128)(2,1)S(1)}, bf16[4,2]{0,1:T(2,128)(2,1)S(1)}, u32[]{:S(2)}, u32[]{:S(2)}) collective-permute-start(bf16[4,2]{0,1:T(2,128)(2,1)S(1)} %collective-permute-done.4), channel_id=1, source_target_pairs={{0,1},{1,2},{2,3},{3,4},{4,5},{5,6},{6,7},{7,8},{8,9},{9,10},{10,1... | collective-permute-start | bytes 56 | tf_op jit(solution)/shard_map/ppermute | solution.py:24
  118.3 5.7 %collective-permute-start.6 = (bf16[4,2]{0,1:T(2,128)(2,1)S(1)}, bf16[4,2]{0,1:T(2,128)(2,1)S(1)}, u32[]{:S(2)}, u32[]{:S(2)}) collective-permute-start(bf16[4,2]{0,1:T(2,128)(2,1)S(1)} %collective-permute-done.5), channel_id=1, source_target_pairs={{0,1},{1,2},{2,3},{3,4},{4,5},{5,6},{6,7},{7,8},{8,9},{9,10},{10,1... | collective-permute-start | bytes 56 | tf_op jit(solution)/shard_map/ppermute | solution.py:24
  124.0 5.7 %collective-permute-start.7 = (bf16[4,2]{0,1:T(2,128)(2,1)S(1)}, bf16[4,2]{0,1:T(2,128)(2,1)S(1)}, u32[]{:S(2)}, u32[]{:S(2)}) collective-permute-start(bf16[4,2]{0,1:T(2,128)(2,1)S(1)} %collective-permute-done.6), channel_id=1, source_target_pairs={{0,1},{1,2},{2,3},{3,4},{4,5},{5,6},{6,7},{7,8},{8,9},{9,10},{10,1... | collective-permute-start | bytes 56 | tf_op jit(solution)/shard_map/ppermute | solution.py:24
  129.7 5.7 %collective-permute-start.8 = (bf16[4,2]{0,1:T(2,128)(2,1)S(1)}, bf16[4,2]{0,1:T(2,128)(2,1)S(1)}, u32[]{:S(2)}, u32[]{:S(2)}) collective-permute-start(bf16[4,2]{0,1:T(2,128)(2,1)S(1)} %collective-permute-done.7), channel_id=1, source_target_pairs={{0,1},{1,2},{2,3},{3,4},{4,5},{5,6},{6,7},{7,8},{8,9},{9,10},{10,1... | collective-permute-start | bytes 56 | tf_op jit(solution)/shard_map/ppermute | solution.py:24
  135.4 5.7 %collective-permute-start.9 = (bf16[4,2]{0,1:T(2,128)(2,1)S(1)}, bf16[4,2]{0,1:T(2,128)(2,1)S(1)}, u32[]{:S(2)}, u32[]{:S(2)}) collective-permute-start(bf16[4,2]{0,1:T(2,128)(2,1)S(1)} %collective-permute-done.8), channel_id=1, source_target_pairs={{0,1},{1,2},{2,3},{3,4},{4,5},{5,6},{6,7},{7,8},{8,9},{9,10},{10,1... | collective-permute-start | bytes 56 | tf_op jit(solution)/shard_map/ppermute | solution.py:24
  141.1 5.7 %collective-permute-start.10 = (bf16[4,2]{0,1:T(2,128)(2,1)S(1)}, bf16[4,2]{0,1:T(2,128)(2,1)S(1)}, u32[]{:S(2)}, u32[]{:S(2)}) collective-permute-start(bf16[4,2]{0,1:T(2,128)(2,1)S(1)} %collective-permute-done.9), channel_id=1, source_target_pairs={{0,1},{1,2},{2,3},{3,4},{4,5},{5,6},{6,7},{7,8},{8,9},{9,10},{10,1... | collective-permute-start | bytes 56 | tf_op jit(solution)/shard_map/ppermute | solution.py:24
  146.8 5.7 %collective-permute-start.11 = (bf16[4,2]{0,1:T(2,128)(2,1)S(1)}, bf16[4,2]{0,1:T(2,128)(2,1)S(1)}, u32[]{:S(2)}, u32[]{:S(2)}) collective-permute-start(bf16[4,2]{0,1:T(2,128)(2,1)S(1)} %collective-permute-done.10), channel_id=1, source_target_pairs={{0,1},{1,2},{2,3},{3,4},{4,5},{5,6},{6,7},{7,8},{8,9},{9,10},{10,1... | collective-permute-start | bytes 56 | tf_op jit(solution)/shard_map/ppermute | solution.py:24
  152.5 5.7 %collective-permute-start.12 = (bf16[4,2]{0,1:T(2,128)(2,1)S(1)}, bf16[4,2]{0,1:T(2,128)(2,1)S(1)}, u32[]{:S(2)}, u32[]{:S(2)}) collective-permute-start(bf16[4,2]{0,1:T(2,128)(2,1)S(1)} %collective-permute-done.11), channel_id=1, source_target_pairs={{0,1},{1,2},{2,3},{3,4},{4,5},{5,6},{6,7},{7,8},{8,9},{9,10},{10,1... | collective-permute-start | bytes 56 | tf_op jit(solution)/shard_map/ppermute | solution.py:24
  158.2 5.7 %collective-permute-start.13 = (bf16[4,2]{0,1:T(2,128)(2,1)S(1)}, bf16[4,2]{0,1:T(2,128)(2,1)S(1)}, u32[]{:S(2)}, u32[]{:S(2)}) collective-permute-start(bf16[4,2]{0,1:T(2,128)(2,1)S(1)} %collective-permute-done.12), channel_id=1, source_target_pairs={{0,1},{1,2},{2,3},{3,4},{4,5},{5,6},{6,7},{7,8},{8,9},{9,10},{10,1... | collective-permute-start | bytes 56 | tf_op jit(solution)/shard_map/ppermute | solution.py:24
  163.9 5.7 %collective-permute-start.14 = (bf16[4,2]{0,1:T(2,128)(2,1)S(1)}, bf16[4,2]{0,1:T(2,128)(2,1)S(1)}, u32[]{:S(2)}, u32[]{:S(2)}) collective-permute-start(bf16[4,2]{0,1:T(2,128)(2,1)S(1)} %collective-permute-done.13), channel_id=1, source_target_pairs={{0,1},{1,2},{2,3},{3,4},{4,5},{5,6},{6,7},{7,8},{8,9},{9,10},{10,1... | collective-permute-start | bytes 56 | tf_op jit(solution)/shard_map/ppermute | solution.py:24
  173.4 10.0 %all-to-all-start = ((f32[16,2,9]{2,1,0:T(2,128)}), f32[16,2,9]{2,1,0:T(2,128)S(1)}, u32[]{:S(2)}, u32[]{:S(2)}) async-start(f32[16,2,9]{2,1,0:T(2,128)} %bitcast.16), calls=%async_computation | async-start | bytes 32768 | tf_op jit(solution)/shard_map/all_to_all | solution.py:148
